TPU v7x, 256 devices: a whole 4x4x8 slice. The times are simulated.
256 devices in a mesh: row: 32 (over y, z), col: 8 (over x, core).
Axes of the slice: x: 4, y: 4, z: 8, core: 2. Of those that a mesh axis runs over, the one named last changes fastest.
Arguments:
- window: float32 [8192, 8192], P('row', 'col'), may hold values from -6 to 6
- leaf_y: float32 [2, 8192, 256], P(None, 'row', 'col'), may hold values from -6 to 6
- tree_y: float32 [2, 5, 8192, 256], P(None, None, 'row', 'col'), may hold values from -6 to 6
Outputs:
- updated: float32 [8192, 8192], P('row', 'col')
All inputs are finite; a program needn't handle non-finite values.
Results may differ from a plain program's by a relative error of at most 0.0003.
Values sent between devices are 32-bit elements; how exact they have to be, the bound alone decides.
A program may use at most 128 MiB of HBM per device.

v0:
```python
import jax
import jax.numpy as jnp
from jax import lax
from jax.experimental import pallas as pl
from jax.experimental.pallas import tpu as pltpu
from jax.sharding import PartitionSpec as P

F32 = jnp.float32
BF16 = jnp.bfloat16
MESH = pl.DeviceIdType.MESH
LEVELS = 5
STEPS = 2 * LEVELS
CHUNKS = 8
GROUPS = 4
LAG = 1
PREP_AT = 3
LEAF = STEPS
SMALL = 32


def full_dot(a, b, ta=False, tb=False):
    dims = (((0,) if ta else (1,), (1,) if tb else (0,)), ((), ()))
    return lax.dot_general(
        a, b, dims, precision=lax.Precision.HIGHEST, preferred_element_type=F32
    )


def half_dot(a, b):
    return jnp.dot(a, b, preferred_element_type=F32)


def split(x):
    high = x.astype(BF16)
    return high, (x - high.astype(F32)).astype(BF16)


def iotas(m, n):
    return (
        lax.broadcasted_iota(jnp.int32, (m, n), 0),
        lax.broadcasted_iota(jnp.int32, (m, n), 1),
    )


def identity(n):
    r, c = iotas(n, n)
    return jnp.where(r == c, 1.0, 0.0)


def spread(blocks):
    s, n = blocks.shape
    r, c = iotas(n, n)
    return jnp.where(r // s == c // s, jnp.concatenate([blocks] * (n // s), axis=0), 0.0)


def fold(matrix, s):
    total = matrix[:s]
    for k in range(1, matrix.shape[0] // s):
        total = total + matrix[k * s : (k + 1) * s]
    return total


def triangle_inverse(gramian):
    n = gramian.shape[0]
    r, c = iotas(n, n)
    diagonal = jnp.where(r == c, gramian, 0.0)
    by_row = 2.0 / jnp.sum(diagonal, axis=1, keepdims=True)
    by_column = 2.0 / jnp.sum(diagonal, axis=0, keepdims=True)
    scaled = jnp.where(r > c, gramian * by_row, 0.0)
    s = SMALL
    power = fold(jnp.where(r // s == c // s, -scaled, 0.0), s)
    rs, cs = iotas(s, n)
    inverse = jnp.where(cs % s == rs, 1.0, 0.0) + power
    power = full_dot(power, spread(power))
    reach = 4
    while reach < s:
        both = full_dot(jnp.concatenate([power, inverse], 0), spread(power))
        power = both[:s]
        inverse = inverse + both[s:]
        reach *= 2
    inverse = inverse + full_dot(inverse, spread(power))
    while s < n // 2:
        corner = fold(
            jnp.where((r // s == c // s + 1) & ((r // s) % 2 == 1), scaled, 0.0), s
        )
        upper = full_dot(corner, spread(inverse))
        after = jnp.concatenate([inverse[:, s:], inverse[:, :s]], axis=1)
        lower = full_dot(after, spread(upper))
        even = (iotas(s, n)[1] // s) % 2 == 0
        inverse = jnp.concatenate(
            [jnp.where(even, inverse, 0.0), jnp.where(even, -lower, inverse)], axis=0
        )
        s *= 2
    first, second = inverse[:, :s], inverse[:, s:]
    lower = full_dot(second, full_dot(scaled[s:, :s], first))
    top = jnp.concatenate([first, jnp.zeros((s, s), F32)], 1)
    return jnp.concatenate([top, jnp.concatenate([-lower, second], 1)], 0) * by_column


def kernel(
    x_ref, own_ref, o_ref, held, came, high, low, wide, far, leaf,
    send_x, recv_x, send_hop, recv_hop, send_own, recv_own, send_far, recv_far,
):
    row, col = lax.axis_index("row"), lax.axis_index("col")
    n_col = lax.axis_size("col")
    part, n = own_ref.shape[1], own_ref.shape[2]
    width = x_ref.shape[1] // CHUNKS

    def partner(level):
        m = level % LEVELS
        s = (
            1 + m + m * (m - 1) // 2 + m * (m - 1) * (m - 2) // 6
            + m * (m - 1) * (m - 2) * (m - 3) // 24
        )
        return (row + s * (1 - 2 * ((row // s) % 2)), col)

    barrier = pltpu.get_barrier_semaphore()
    for level in range(LEVELS):
        pl.semaphore_signal(barrier, inc=1, device_id=partner(level), device_id_type=MESH)
    for d in range(1, n_col):
        pl.semaphore_signal(
            barrier, inc=1, device_id=(row, (col + d) % n_col), device_id_type=MESH
        )
    pl.semaphore_wait(barrier, LEVELS + n_col - 1)

    def columns(q):
        return pl.ds(pl.multiple_of(q * width, width), width)

    def exchange(source, level, q):
        return pltpu.make_async_remote_copy(
            src_ref=source.at[:, columns(q)],
            dst_ref=came.at[level, :, columns(q)],
            send_sem=send_x.at[level, q],
            recv_sem=recv_x.at[level, q],
            device_id=partner(level),
            device_id_type=MESH,
        )

    def hop(stage, level):
        return pltpu.make_async_remote_copy(
            src_ref=own_ref.at[stage],
            dst_ref=far.at[stage],
            send_sem=send_hop.at[stage],
            recv_sem=recv_hop.at[stage],
            device_id=partner(level),
            device_id_type=MESH,
        )

    mine = pl.ds(pl.multiple_of(col * part, part), part)

    def share(source, stage, lanes, send, recv):
        wide[stage, mine, lanes] = source[stage]

        def one(d, _):
            pltpu.make_async_remote_copy(
                src_ref=source.at[stage],
                dst_ref=wide.at[stage, mine, lanes],
                send_sem=send.at[stage],
                recv_sem=recv.at[stage],
                device_id=(row, (col + d) % n_col),
                device_id_type=MESH,
            ).start()
            return 0

        lax.fori_loop(1, n_col, one, 0)

    own_lanes, far_lanes = pl.ds(0, n), pl.ds(n, n)

    def all_shared(stage, lanes, send, recv):
        rows = pl.ds(0, (n_col - 1) * part)
        return pltpu.make_async_remote_copy(
            src_ref=wide.at[stage, rows, lanes],
            dst_ref=wide.at[stage, rows, lanes],
            send_sem=send.at[stage],
            recv_sem=recv.at[stage],
            device_id=(row, (col + 1) % n_col),
            device_id_type=MESH,
        )

    def share_own(stage):
        share(own_ref, stage, own_lanes, send_own, recv_own)

    def share_far(stage):
        hop(stage, 0).wait_recv()
        share(far, stage, far_lanes, send_far, recv_far)

    def leaf_reflection(i):
        lanes = pl.ds(pl.multiple_of((i % 2) * n, n), n)
        w = wide[LEAF + i // 2, :, lanes]
        inverse = triangle_inverse(full_dot(w, w, False, True))
        leaf[i] = identity(n) - full_dot(full_dot(w, inverse, True, False), w)

    hop(LEAF, 0).start()
    hop(0, 0).start()
    share_own(LEAF)

    def start_hop(stage, _):
        hop(stage, stage).start()
        return 0

    lax.fori_loop(1, STEPS, start_hop, 0)

    def start_window(q, _):
        exchange(x_ref, 0, q).start()
        return 0

    lax.fori_loop(0, CHUNKS, start_window, 0)
    share_far(LEAF)
    share_own(0)
    share_far(0)
    held[0] = x_ref[...]

    all_shared(LEAF, own_lanes, send_own, recv_own).wait_recv()

    def start_leaf(i, _):
        leaf_reflection(i)

        @pl.when(i == 0)
        def _():
            def rest(stage, _):
                share_own(stage)
                share_far(stage)
                return 0

            lax.fori_loop(1, LEVELS, rest, 0)
            share_own(LEAF + 1)
            lax.fori_loop(LEVELS, STEPS, rest, 0)
            all_shared(LEAF, far_lanes, send_far, recv_far).wait_recv()

        return 0

    lax.fori_loop(0, 2, start_leaf, 0)

    def prepare(level):
        all_shared(level, own_lanes, send_own, recv_own).wait_recv()
        all_shared(level, far_lanes, send_far, recv_far).wait_recv()
        both = wide[level]
        inverse = triangle_inverse(full_dot(both, both, False, True))
        out = full_dot(full_dot(both[:, :n], inverse, True, False), both)
        near, other = identity(n) - out[:, :n], -out[:, n:]

        def keep(lanes, matrix):
            high[level, :, lanes], low[level, :, lanes] = split(matrix)

        keep(own_lanes, near)
        keep(far_lanes, other)

        @pl.when(level == 0)
        def _():
            keep(own_lanes, full_dot(near, leaf[0]))
            keep(far_lanes, full_dot(other, leaf[1]))

        @pl.when(level == LEVELS - 1)
        def _():
            all_shared(LEAF + 1, own_lanes, send_own, recv_own).wait_recv()
            leaf_reflection(2)
            keep(own_lanes, full_dot(leaf[2], near))
            keep(far_lanes, full_dot(leaf[2], other))

    def advance(level, q):
        exchange(x_ref, level, q).wait_recv()
        both = jnp.concatenate(
            [held[level, :, columns(q)], came[level, :, columns(q)]], axis=0
        )
        both_high, both_low = split(both)
        out = half_dot(high[level], both_high) + (
            half_dot(high[level], both_low) + half_dot(low[level], both_high)
        )

        @pl.when(level == STEPS - 1)
        def _():
            o_ref[:, columns(q)] = out

        @pl.when(level < STEPS - 1)
        def _():
            held[level + 1, :, columns(q)] = out
            exchange(held.at[level + 1], level + 1, q).start()

    def wave(u, _):
        def item(q, _):
            level = u - 1 - LAG * (q // (CHUNKS // GROUPS))

            @pl.when((level >= 0) & (level < STEPS))
            def _():
                advance(level, q)

            return 0

        lax.fori_loop(0, PREP_AT, item, 0)

        @pl.when(u < STEPS)
        def _():
            prepare(u)

        lax.fori_loop(PREP_AT, CHUNKS, item, 0)
        return 0

    lax.fori_loop(0, STEPS + LAG * (GROUPS - 1) + 1, wave, 0)

    def drain_x(level, _):
        def one(q, _):
            exchange(x_ref, level, q).wait_send()
            return 0

        return lax.fori_loop(0, CHUNKS, one, 0)

    lax.fori_loop(0, STEPS, drain_x, 0)

    def drain_shares(stage, _):
        hop(stage, 0).wait_send()
        all_shared(stage, own_lanes, send_own, recv_own).wait_send()
        all_shared(stage, far_lanes, send_far, recv_far).wait_send()
        return 0

    lax.fori_loop(0, STEPS + 1, drain_shares, 0)
    all_shared(LEAF + 1, own_lanes, send_own, recv_own).wait_send()


def per_device(window, leaf_y, tree_y):
    rows, width = window.shape
    n, part = tree_y.shape[2:]
    own = jnp.concatenate([tree_y.reshape(STEPS, n, part), leaf_y], 0)
    own = jnp.swapaxes(own, 1, 2)
    dma = pltpu.SemaphoreType.DMA
    return pl.pallas_call(
        kernel,
        out_shape=jax.ShapeDtypeStruct(window.shape, F32),
        in_specs=[pl.BlockSpec(memory_space=pltpu.VMEM)] * 2,
        out_specs=pl.BlockSpec(memory_space=pltpu.VMEM),
        scratch_shapes=[
            pltpu.VMEM((STEPS, rows, width), F32),
            pltpu.VMEM((STEPS, rows, width), F32),
            pltpu.VMEM((STEPS, n, 2 * n), BF16),
            pltpu.VMEM((STEPS, n, 2 * n), BF16),
            pltpu.VMEM((STEPS + 2, n, 2 * n), F32),
            pltpu.VMEM((STEPS + 1, part, n), F32),
            pltpu.VMEM((3, n, n), F32),
            dma((STEPS, CHUNKS)),
            dma((STEPS, CHUNKS)),
            dma((STEPS + 1,)),
            dma((STEPS + 1,)),
            dma((STEPS + 2,)),
            dma((STEPS + 2,)),
            dma((STEPS + 1,)),
            dma((STEPS + 1,)),
        ],
        compiler_params=pltpu.CompilerParams(
            collective_id=0, has_side_effects=True, vmem_limit_bytes=56 * 2**20
        ),
        name="panels",
    )(window, own)


def solution(mesh):
    return jax.shard_map(
        per_device,
        mesh=mesh,
        in_specs=(P("row", "col"), P(None, "row", "col"), P(None, None, "row", "col")),
        out_specs=P("row", "col"),
        check_vma=False,
    )
```

profile of v0, /device:TPU:8, one launch (start us, length us, event | category | flops | bytes accessed | tf_op | source)
XLA Modules:
  0.0 246.9 jit_solution(11309431205381946979)
XLA Ops:
  0.0 1.8 maximum_bitcast_fusion.own_ref
  1.8 242.8 %panels.1 = f32[256,1024]{1,0:T(8,128)} custom-call(f32[256,1024]{1,0:T(8,128)} %x_ref.1, f32[12,32,256]{2,1,0:T(8,128)} %maximum_bitcast_fusion.own_ref), custom_call_target="tpu_custom_call" | custom-call | tf_op jit(solution)/shard_map/panels/pallas_call | solution.py:324
  244.6 2.3 copy.5
where the time goes:
time: 250 us; the launch traced here: 247 us
  Pallas kernels  243 us (97%)
    pallas_call x1, Pallas kernels, per_device(): pl.pallas_call(kernel, out_shape=jax.ShapeDtypeStruct(window.shape, F32),...  243 us

commit v1 on v0

--- a/solution.py
+++ b/solution.py
@@ -16,6 +16,23 @@
 PREP_AT = 3
 LEAF = STEPS
 SMALL = 32
+TURN = 2
+TURNS = (TURN, TURN + LEVELS)
+SWAPS = (TURN, TURN + LEVELS + 1)
+EXTRA = {3: (11, 12), 4: (13, 14), 11: (15, None), 5: (16, 17), 6: (18, 19)}
+SLOTS = 20
+
+
+def at_least(value, bound):
+    return (value + 32 - bound) // 32
+
+
+def equal(value, bound):
+    return at_least(value, bound) - at_least(value, bound + 1)
+
+
+def core_level(level):
+    return equal(level, TURNS[0]) + equal(level, TURNS[1])
 
 
 def full_dot(a, b, ta=False, tb=False):
@@ -98,29 +115,41 @@
 
 def kernel(
     x_ref, own_ref, o_ref, held, came, high, low, wide, far, leaf,
-    send_x, recv_x, send_hop, recv_hop, send_own, recv_own, send_far, recv_far,
+    send_x, recv_x, send_swap, recv_swap, send_hop, recv_hop,
+    send_near, recv_near, send_far, recv_far,
 ):
     row, col = lax.axis_index("row"), lax.axis_index("col")
     n_col = lax.axis_size("col")
     part, n = own_ref.shape[1], own_ref.shape[2]
     width = x_ref.shape[1] // CHUNKS
 
-    def partner(level):
-        m = level % LEVELS
+    def towards(m):
         s = (
             1 + m + m * (m - 1) // 2 + m * (m - 1) * (m - 2) // 6
             + m * (m - 1) * (m - 2) * (m - 3) // 24
         )
-        return (row + s * (1 - 2 * ((row // s) % 2)), col)
-
+        return s * (1 - 2 * ((row // s) % 2))
+
+    def moved_of(any_col):
+        return ((row // 2**TURN) % 2 + any_col) % 2
+
+    moved = moved_of(col)
+    sibling = col + 1 - 2 * (col % 2)
+    across = row + towards(TURN)
+
+    def partner(level):
+        return (
+            row + (1 - core_level(level)) * towards(level % LEVELS),
+            col + core_level(level) * (sibling - col),
+        )
+
+    greeted = [(row + towards(m), col) for m in range(LEVELS)]
+    greeted += [(across + towards(m), col) for m in range(LEVELS) if m != TURN]
+    greeted += [(across, sibling)] + [(row, (col + d) % n_col) for d in range(1, n_col)]
     barrier = pltpu.get_barrier_semaphore()
-    for level in range(LEVELS):
-        pl.semaphore_signal(barrier, inc=1, device_id=partner(level), device_id_type=MESH)
-    for d in range(1, n_col):
-        pl.semaphore_signal(
-            barrier, inc=1, device_id=(row, (col + d) % n_col), device_id_type=MESH
-        )
-    pl.semaphore_wait(barrier, LEVELS + n_col - 1)
+    for other in greeted:
+        pl.semaphore_signal(barrier, inc=1, device_id=other, device_id_type=MESH)
+    pl.semaphore_wait(barrier, len(greeted))
 
     def columns(q):
         return pl.ds(pl.multiple_of(q * width, width), width)
@@ -135,35 +164,94 @@
             device_id_type=MESH,
         )
 
-    def hop(stage, level):
+    def swap(way, q):
+        return pltpu.make_async_remote_copy(
+            src_ref=held.at[SWAPS[0] + way * (SWAPS[1] - SWAPS[0]), :, columns(q)],
+            dst_ref=held.at[STEPS + way, :, columns(q)],
+            send_sem=send_swap.at[way, q],
+            recv_sem=recv_swap.at[way, q],
+            device_id=(across, sibling),
+            device_id_type=MESH,
+        )
+
+    def hop(stage, slot, to_row):
         return pltpu.make_async_remote_copy(
             src_ref=own_ref.at[stage],
-            dst_ref=far.at[stage],
-            send_sem=send_hop.at[stage],
-            recv_sem=recv_hop.at[stage],
-            device_id=partner(level),
+            dst_ref=far.at[slot],
+            send_sem=send_hop.at[slot],
+            recv_sem=recv_hop.at[slot],
+            device_id=(to_row, col),
             device_id_type=MESH,
         )
 
     mine = pl.ds(pl.multiple_of(col * part, part), part)
-
-    def share(source, stage, lanes, send, recv):
-        wide[stage, mine, lanes] = source[stage]
-
-        def one(d, _):
+    near_lanes, far_lanes = pl.ds(0, n), pl.ds(n, n)
+
+    def share(stage, lanes, kept, other, send, recv):
+        def to(source, d):
             pltpu.make_async_remote_copy(
-                src_ref=source.at[stage],
+                src_ref=source,
                 dst_ref=wide.at[stage, mine, lanes],
                 send_sem=send.at[stage],
                 recv_sem=recv.at[stage],
                 device_id=(row, (col + d) % n_col),
                 device_id_type=MESH,
             ).start()
+
+        def one(d, _):
+            if other is None:
+                to(kept, d)
+            else:
+                away = moved_of(col + d)
+
+                @pl.when(away == 0)
+                def _():
+                    to(kept, d)
+
+                @pl.when(away == 1)
+                def _():
+                    to(other, d)
+
             return 0
 
         lax.fori_loop(1, n_col, one, 0)
-
-    own_lanes, far_lanes = pl.ds(0, n), pl.ds(n, n)
+        if other is None:
+            wide[stage, mine, lanes] = kept[...]
+        else:
+
+            @pl.when(moved == 0)
+            def _():
+                wide[stage, mine, lanes] = kept[...]
+
+            @pl.when(moved == 1)
+            def _():
+                wide[stage, mine, lanes] = other[...]
+
+    def arrive(slot):
+        hop(0, slot, row + towards(0)).wait_recv()
+
+    def share_both(stage):
+        own = own_ref.at[stage]
+        if stage == LEAF + 1:
+            arrive(EXTRA[stage][0])
+            share(stage, near_lanes, own, far.at[EXTRA[stage][0]], send_near, recv_near)
+            return
+        if stage in EXTRA:
+            near_slot, far_slot = EXTRA[stage]
+            arrive(near_slot)
+            share(stage, near_lanes, own, far.at[near_slot], send_near, recv_near)
+            arrive(stage)
+            arrive(far_slot)
+            share(stage, far_lanes, far.at[stage], far.at[far_slot], send_far, recv_far)
+            return
+        if stage in TURNS:
+            arrive(stage)
+            share(stage, near_lanes, own, far.at[stage], send_near, recv_near)
+            share(stage, far_lanes, far.at[stage], own, send_far, recv_far)
+            return
+        share(stage, near_lanes, own, None, send_near, recv_near)
+        arrive(stage)
+        share(stage, far_lanes, far.at[stage], None, send_far, recv_far)
 
     def all_shared(stage, lanes, send, recv):
         rows = pl.ds(0, (n_col - 1) * part)
@@ -172,16 +260,9 @@
             dst_ref=wide.at[stage, rows, lanes],
             send_sem=send.at[stage],
             recv_sem=recv.at[stage],
-            device_id=(row, (col + 1) % n_col),
+            device_id=(row, sibling),
             device_id_type=MESH,
         )
-
-    def share_own(stage):
-        share(own_ref, stage, own_lanes, send_own, recv_own)
-
-    def share_far(stage):
-        hop(stage, 0).wait_recv()
-        share(far, stage, far_lanes, send_far, recv_far)
 
     def leaf_reflection(i):
         lanes = pl.ds(pl.multiple_of((i % 2) * n, n), n)
@@ -189,41 +270,36 @@
         inverse = triangle_inverse(full_dot(w, w, False, True))
         leaf[i] = identity(n) - full_dot(full_dot(w, inverse, True, False), w)
 
-    hop(LEAF, 0).start()
-    hop(0, 0).start()
-    share_own(LEAF)
-
-    def start_hop(stage, _):
-        hop(stage, stage).start()
-        return 0
-
-    lax.fori_loop(1, STEPS, start_hop, 0)
+    hop(LEAF, LEAF, row + towards(0)).start()
+    hop(0, 0, row + towards(0)).start()
+    share(LEAF, near_lanes, own_ref.at[LEAF], None, send_near, recv_near)
+    for stage in (1, 2, 7, 8, 9):
+        hop(stage, stage, row + towards(stage % LEVELS)).start()
 
     def start_window(q, _):
         exchange(x_ref, 0, q).start()
         return 0
 
     lax.fori_loop(0, CHUNKS, start_window, 0)
-    share_far(LEAF)
-    share_own(0)
-    share_far(0)
+    arrive(LEAF)
+    share(LEAF, far_lanes, far.at[LEAF], None, send_far, recv_far)
+    share_both(0)
+    for stage, slots in EXTRA.items():
+        hop(stage, slots[0], across).start()
+        if stage < STEPS:
+            hop(stage, stage, row + towards(stage % LEVELS)).start()
+            hop(stage, slots[1], across + towards(stage % LEVELS)).start()
     held[0] = x_ref[...]
 
-    all_shared(LEAF, own_lanes, send_own, recv_own).wait_recv()
+    all_shared(LEAF, near_lanes, send_near, recv_near).wait_recv()
 
     def start_leaf(i, _):
         leaf_reflection(i)
 
         @pl.when(i == 0)
         def _():
-            def rest(stage, _):
-                share_own(stage)
-                share_far(stage)
-                return 0
-
-            lax.fori_loop(1, LEVELS, rest, 0)
-            share_own(LEAF + 1)
-            lax.fori_loop(LEVELS, STEPS, rest, 0)
+            for stage in (1, 2, 7, 8, 9):
+                share_both(stage)
             all_shared(LEAF, far_lanes, send_far, recv_far).wait_recv()
 
         return 0
@@ -231,7 +307,7 @@
     lax.fori_loop(0, 2, start_leaf, 0)
 
     def prepare(level):
-        all_shared(level, own_lanes, send_own, recv_own).wait_recv()
+        all_shared(level, near_lanes, send_near, recv_near).wait_recv()
         all_shared(level, far_lanes, send_far, recv_far).wait_recv()
         both = wide[level]
         inverse = triangle_inverse(full_dot(both, both, False, True))
@@ -241,30 +317,35 @@
         def keep(lanes, matrix):
             high[level, :, lanes], low[level, :, lanes] = split(matrix)
 
-        keep(own_lanes, near)
+        keep(near_lanes, near)
         keep(far_lanes, other)
 
         @pl.when(level == 0)
         def _():
-            keep(own_lanes, full_dot(near, leaf[0]))
+            keep(near_lanes, full_dot(near, leaf[0]))
             keep(far_lanes, full_dot(other, leaf[1]))
 
         @pl.when(level == LEVELS - 1)
         def _():
-            all_shared(LEAF + 1, own_lanes, send_own, recv_own).wait_recv()
+            all_shared(LEAF + 1, near_lanes, send_near, recv_near).wait_recv()
             leaf_reflection(2)
-            keep(own_lanes, full_dot(leaf[2], near))
+            keep(near_lanes, full_dot(leaf[2], near))
             keep(far_lanes, full_dot(leaf[2], other))
 
     def advance(level, q):
         exchange(x_ref, level, q).wait_recv()
+        slot = level + moved * (
+            equal(level, SWAPS[0]) * (STEPS - SWAPS[0])
+            + equal(level, SWAPS[1]) * (STEPS + 1 - SWAPS[1])
+        )
         both = jnp.concatenate(
-            [held[level, :, columns(q)], came[level, :, columns(q)]], axis=0
+            [held[slot, :, columns(q)], came[level, :, columns(q)]], axis=0
         )
         both_high, both_low = split(both)
         out = half_dot(high[level], both_high) + (
             half_dot(high[level], both_low) + half_dot(low[level], both_high)
         )
+        swaps = moved * (equal(level, SWAPS[0] - 1) + equal(level, SWAPS[1] - 1))
 
         @pl.when(level == STEPS - 1)
         def _():
@@ -273,28 +354,60 @@
         @pl.when(level < STEPS - 1)
         def _():
             held[level + 1, :, columns(q)] = out
-            exchange(held.at[level + 1], level + 1, q).start()
+
+            @pl.when(swaps == 0)
+            def _():
+                exchange(held.at[level + 1], level + 1, q).start()
+
+            @pl.when(swaps == 1)
+            def _():
+                swap(equal(level, SWAPS[1] - 1), q).start()
+
+    def settle(way, q):
+        @pl.when(moved == 1)
+        def _():
+            swap(way, q).wait_recv()
+            exchange(held.at[STEPS + way], SWAPS[0] + way * (SWAPS[1] - SWAPS[0]), q).start()
+
+    def item(step, q):
+        way = at_least(step, SWAPS[1] + 1)
+        level = step - at_least(step, SWAPS[0] + 1) - at_least(step, SWAPS[1] + 2)
+        swapping = equal(step, SWAPS[0]) + equal(step, SWAPS[1] + 1)
+
+        @pl.when(swapping == 1)
+        def _():
+            settle(way, q)
+
+        @pl.when(swapping == 0)
+        def _():
+            advance(level, q)
 
     def wave(u, _):
-        def item(q, _):
-            level = u - 1 - LAG * (q // (CHUNKS // GROUPS))
-
-            @pl.when((level >= 0) & (level < STEPS))
+        def one(q, _):
+            step = u - 1 - LAG * (q // (CHUNKS // GROUPS))
+
+            @pl.when((step >= 0) & (step < STEPS + 2))
             def _():
-                advance(level, q)
+                item(step, q)
 
             return 0
 
-        lax.fori_loop(0, PREP_AT, item, 0)
-
-        @pl.when(u < STEPS)
-        def _():
-            prepare(u)
-
-        lax.fori_loop(PREP_AT, CHUNKS, item, 0)
+        lax.fori_loop(0, PREP_AT, one, 0)
+        swapping = equal(u, SWAPS[0]) + equal(u, SWAPS[1] + 1)
+
+        @pl.when((u < STEPS + 2) & (swapping == 0))
+        def _():
+            prepare(u - at_least(u, SWAPS[0] + 1) - at_least(u, SWAPS[1] + 2))
+
+        @pl.when(u == SWAPS[0])
+        def _():
+            for stage in EXTRA:
+                share_both(stage)
+
+        lax.fori_loop(PREP_AT, CHUNKS, one, 0)
         return 0
 
-    lax.fori_loop(0, STEPS + LAG * (GROUPS - 1) + 1, wave, 0)
+    lax.fori_loop(0, STEPS + 2 + LAG * (GROUPS - 1) + 1, wave, 0)
 
     def drain_x(level, _):
         def one(q, _):
@@ -305,14 +418,28 @@
 
     lax.fori_loop(0, STEPS, drain_x, 0)
 
+    @pl.when(moved == 1)
+    def _():
+        def drain_swap(q, _):
+            swap(0, q).wait_send()
+            swap(1, q).wait_send()
+            return 0
+
+        lax.fori_loop(0, CHUNKS, drain_swap, 0)
+
+    def drain_hop(slot, _):
+        hop(0, slot, row + towards(0)).wait_send()
+        return 0
+
+    lax.fori_loop(0, SLOTS, drain_hop, 0)
+
     def drain_shares(stage, _):
-        hop(stage, 0).wait_send()
-        all_shared(stage, own_lanes, send_own, recv_own).wait_send()
+        all_shared(stage, near_lanes, send_near, recv_near).wait_send()
         all_shared(stage, far_lanes, send_far, recv_far).wait_send()
         return 0
 
     lax.fori_loop(0, STEPS + 1, drain_shares, 0)
-    all_shared(LEAF + 1, own_lanes, send_own, recv_own).wait_send()
+    all_shared(LEAF + 1, near_lanes, send_near, recv_near).wait_send()
 
 
 def per_device(window, leaf_y, tree_y):
@@ -327,21 +454,23 @@
         in_specs=[pl.BlockSpec(memory_space=pltpu.VMEM)] * 2,
         out_specs=pl.BlockSpec(memory_space=pltpu.VMEM),
         scratch_shapes=[
-            pltpu.VMEM((STEPS, rows, width), F32),
+            pltpu.VMEM((STEPS + 2, rows, width), F32),
             pltpu.VMEM((STEPS, rows, width), F32),
             pltpu.VMEM((STEPS, n, 2 * n), BF16),
             pltpu.VMEM((STEPS, n, 2 * n), BF16),
             pltpu.VMEM((STEPS + 2, n, 2 * n), F32),
-            pltpu.VMEM((STEPS + 1, part, n), F32),
+            pltpu.VMEM((SLOTS, part, n), F32),
             pltpu.VMEM((3, n, n), F32),
             dma((STEPS, CHUNKS)),
             dma((STEPS, CHUNKS)),
-            dma((STEPS + 1,)),
-            dma((STEPS + 1,)),
+            dma((2, CHUNKS)),
+            dma((2, CHUNKS)),
+            dma((SLOTS,)),
+            dma((SLOTS,)),
             dma((STEPS + 2,)),
             dma((STEPS + 2,)),
-            dma((STEPS + 1,)),
-            dma((STEPS + 1,)),
+            dma((STEPS + 2,)),
+            dma((STEPS + 2,)),
         ],
         compiler_params=pltpu.CompilerParams(
             collective_id=0, has_side_effects=True, vmem_limit_bytes=56 * 2**20

time: 250 us -> 242 us (0.968)
  Pallas kernels: 243 us -> 236 us
    pallas_call x1, Pallas kernels: 243 us -> 236 us  [per_device(): pl.pallas_call(kernel, out_shape=jax.ShapeDtypeStruct(window.shape, F32),...]
where the time goes in v1:
time: 242 us; the launch traced here: 240 us
  Pallas kernels  236 us (98%)
    pallas_call x1, Pallas kernels, per_device(): pl.pallas_call(kernel, out_shape=jax.ShapeDtypeStruct(window.shape, F32),...  236 us

profile of v1, /device:TPU:8, one launch (start us, length us, event | category | flops | bytes accessed | tf_op | source)
XLA Modules:
  0.0 240.1 jit_solution(9349989812510980556)
XLA Ops:
  0.0 1.8 maximum_bitcast_fusion.own_ref
  1.8 236.0 %panels.1 = f32[256,1024]{1,0:T(8,128)} custom-call(f32[256,1024]{1,0:T(8,128)} %x_ref.1, f32[12,32,256]{2,1,0:T(8,128)} %maximum_bitcast_fusion.own_ref), custom_call_target="tpu_custom_call" | custom-call | tf_op jit(solution)/shard_map/panels/pallas_call | solution.py:451
  237.7 2.3 copy.5

commit v2 on v1

--- a/solution.py
+++ b/solution.py
@@ -11,9 +11,13 @@
 LEVELS = 5
 STEPS = 2 * LEVELS
 CHUNKS = 8
-GROUPS = 4
-LAG = 1
-PREP_AT = 3
+ORDER = (
+    16648, 21397905, 25740427, 58835603, 12878356, 44649885,
+    63132204, 80447502, 111793807, 98945817, 65902647, 84283710,
+    68279353, 138960945, 158356681, 89122091, 110008648, 125085904,
+    160487892, 191962835, 127364429, 181824220, 165126854, 184135631,
+    202781283, 221918177, 268432741,
+)
 LEAF = STEPS
 SMALL = 32
 TURN = 2
@@ -114,13 +118,13 @@
 
 
 def kernel(
-    x_ref, own_ref, o_ref, held, came, high, low, wide, far, leaf,
+    x_ref, tree_ref, leaf_ref, o_ref, held, came, high, low, wide, far, leaf,
     send_x, recv_x, send_swap, recv_swap, send_hop, recv_hop,
-    send_near, recv_near, send_far, recv_far,
+    send_near, recv_near, send_far, recv_far, send_leaf, recv_leaf,
 ):
     row, col = lax.axis_index("row"), lax.axis_index("col")
     n_col = lax.axis_size("col")
-    part, n = own_ref.shape[1], own_ref.shape[2]
+    part, n = leaf_ref.shape[1:]
     width = x_ref.shape[1] // CHUNKS
 
     def towards(m):
@@ -174,9 +178,14 @@
             device_id_type=MESH,
         )
 
+    def own(stage):
+        if stage < LEAF:
+            return tree_ref.at[stage // LEVELS, stage % LEVELS]
+        return leaf_ref.at[stage - LEAF]
+
     def hop(stage, slot, to_row):
         return pltpu.make_async_remote_copy(
-            src_ref=own_ref.at[stage],
+            src_ref=own(stage),
             dst_ref=far.at[slot],
             send_sem=send_hop.at[slot],
             recv_sem=recv_hop.at[slot],
@@ -231,25 +240,24 @@
         hop(0, slot, row + towards(0)).wait_recv()
 
     def share_both(stage):
-        own = own_ref.at[stage]
         if stage == LEAF + 1:
             arrive(EXTRA[stage][0])
-            share(stage, near_lanes, own, far.at[EXTRA[stage][0]], send_near, recv_near)
+            share(stage, near_lanes, own(stage), far.at[EXTRA[stage][0]], send_near, recv_near)
             return
         if stage in EXTRA:
             near_slot, far_slot = EXTRA[stage]
             arrive(near_slot)
-            share(stage, near_lanes, own, far.at[near_slot], send_near, recv_near)
+            share(stage, near_lanes, own(stage), far.at[near_slot], send_near, recv_near)
             arrive(stage)
             arrive(far_slot)
             share(stage, far_lanes, far.at[stage], far.at[far_slot], send_far, recv_far)
             return
         if stage in TURNS:
             arrive(stage)
-            share(stage, near_lanes, own, far.at[stage], send_near, recv_near)
-            share(stage, far_lanes, far.at[stage], own, send_far, recv_far)
+            share(stage, near_lanes, own(stage), far.at[stage], send_near, recv_near)
+            share(stage, far_lanes, far.at[stage], own(stage), send_far, recv_far)
             return
-        share(stage, near_lanes, own, None, send_near, recv_near)
+        share(stage, near_lanes, own(stage), None, send_near, recv_near)
         arrive(stage)
         share(stage, far_lanes, far.at[stage], None, send_far, recv_far)
 
@@ -272,7 +280,7 @@
 
     hop(LEAF, LEAF, row + towards(0)).start()
     hop(0, 0, row + towards(0)).start()
-    share(LEAF, near_lanes, own_ref.at[LEAF], None, send_near, recv_near)
+    share(LEAF, near_lanes, own(LEAF), None, send_near, recv_near)
     for stage in (1, 2, 7, 8, 9):
         hop(stage, stage, row + towards(stage % LEVELS)).start()
 
@@ -291,20 +299,36 @@
             hop(stage, slots[1], across + towards(stage % LEVELS)).start()
     held[0] = x_ref[...]
 
-    all_shared(LEAF, near_lanes, send_near, recv_near).wait_recv()
-
-    def start_leaf(i, _):
-        leaf_reflection(i)
-
-        @pl.when(i == 0)
-        def _():
-            for stage in (1, 2, 7, 8, 9):
-                share_both(stage)
-            all_shared(LEAF, far_lanes, send_far, recv_far).wait_recv()
-
-        return 0
-
-    lax.fori_loop(0, 2, start_leaf, 0)
+    share_both(1)
+
+    core = col % 2
+
+    @pl.when(core == 0)
+    def _():
+        all_shared(LEAF, near_lanes, send_near, recv_near).wait_recv()
+
+    @pl.when(core == 1)
+    def _():
+        all_shared(LEAF, far_lanes, send_far, recv_far).wait_recv()
+
+    leaf_reflection(core)
+    to_sibling = pltpu.make_async_remote_copy(
+        src_ref=leaf.at[core],
+        dst_ref=leaf.at[core],
+        send_sem=send_leaf,
+        recv_sem=recv_leaf,
+        device_id=(row, sibling),
+        device_id_type=MESH,
+    )
+    to_sibling.start()
+
+    @pl.when(core == 1)
+    def _():
+        all_shared(LEAF, near_lanes, send_near, recv_near).wait_recv()
+
+    @pl.when(core == 0)
+    def _():
+        all_shared(LEAF, far_lanes, send_far, recv_far).wait_recv()
 
     def prepare(level):
         all_shared(level, near_lanes, send_near, recv_near).wait_recv()
@@ -322,6 +346,7 @@
 
         @pl.when(level == 0)
         def _():
+            to_sibling.wait()
             keep(near_lanes, full_dot(near, leaf[0]))
             keep(far_lanes, full_dot(other, leaf[1]))
 
@@ -382,32 +407,39 @@
         def _():
             advance(level, q)
 
-    def wave(u, _):
-        def one(q, _):
-            step = u - 1 - LAG * (q // (CHUNKS // GROUPS))
-
-            @pl.when((step >= 0) & (step < STEPS + 2))
+    def turn(w, _):
+        word = jnp.int32(0)
+        for k, entries in enumerate(ORDER):
+            word = jnp.where(w == k, jnp.int32(entries), word)
+
+        def one(_, left):
+            entry = lax.rem(left, 128)
+            what, count = lax.rem(entry, 9), lax.div(entry, 9)
+
+            @pl.when((what < 8) & (count < STEPS + 2))
             def _():
-                item(step, q)
-
-            return 0
-
-        lax.fori_loop(0, PREP_AT, one, 0)
-        swapping = equal(u, SWAPS[0]) + equal(u, SWAPS[1] + 1)
-
-        @pl.when((u < STEPS + 2) & (swapping == 0))
-        def _():
-            prepare(u - at_least(u, SWAPS[0] + 1) - at_least(u, SWAPS[1] + 2))
-
-        @pl.when(u == SWAPS[0])
-        def _():
-            for stage in EXTRA:
-                share_both(stage)
-
-        lax.fori_loop(PREP_AT, CHUNKS, one, 0)
+                item(count, what)
+
+            @pl.when((what == 8) & (count < STEPS))
+            def _():
+                @pl.when(count == 1)
+                def _():
+                    for stage in (2, 7, 8, 9):
+                        share_both(stage)
+
+                @pl.when(count == TURN)
+                def _():
+                    for stage in EXTRA:
+                        share_both(stage)
+
+                prepare(count)
+
+            return lax.div(left, 128)
+
+        lax.fori_loop(0, 4, one, word)
         return 0
 
-    lax.fori_loop(0, STEPS + 2 + LAG * (GROUPS - 1) + 1, wave, 0)
+    lax.fori_loop(0, len(ORDER), turn, 0)
 
     def drain_x(level, _):
         def one(q, _):
@@ -445,13 +477,11 @@
 def per_device(window, leaf_y, tree_y):
     rows, width = window.shape
     n, part = tree_y.shape[2:]
-    own = jnp.concatenate([tree_y.reshape(STEPS, n, part), leaf_y], 0)
-    own = jnp.swapaxes(own, 1, 2)
     dma = pltpu.SemaphoreType.DMA
     return pl.pallas_call(
         kernel,
         out_shape=jax.ShapeDtypeStruct(window.shape, F32),
-        in_specs=[pl.BlockSpec(memory_space=pltpu.VMEM)] * 2,
+        in_specs=[pl.BlockSpec(memory_space=pltpu.VMEM)] * 3,
         out_specs=pl.BlockSpec(memory_space=pltpu.VMEM),
         scratch_shapes=[
             pltpu.VMEM((STEPS + 2, rows, width), F32),
@@ -471,12 +501,14 @@
             dma((STEPS + 2,)),
             dma((STEPS + 2,)),
             dma((STEPS + 2,)),
+            dma,
+            dma,
         ],
         compiler_params=pltpu.CompilerParams(
             collective_id=0, has_side_effects=True, vmem_limit_bytes=56 * 2**20
         ),
         name="panels",
-    )(window, own)
+    )(window, jnp.swapaxes(tree_y, 2, 3), jnp.swapaxes(leaf_y, 1, 2))
 
 
 def solution(mesh):

time: 242 us -> 220 us (0.909)
  the two profiles are of different devices: /device:TPU:8 before, /device:TPU:3 now
where the time goes in v2:
time: 220 us
  Pallas kernels  218 us (99%)
  local copies, waits for them, and re-layouts  2.31 us (1%)
    pallas_call x1, Pallas kernels, per_device(): pl.pallas_call(kernel, out_shape=jax.ShapeDtypeStruct(window.shape, F32),...  218 us

profile of v2, /device:TPU:3, one launch (start us, length us, event | category | flops | bytes accessed | tf_op | source)
XLA Modules:
  0.0 220.0 jit_solution(13174619952924317180)
XLA Ops:
  0.0 217.7 %panels.1 = f32[256,1024]{1,0:T(8,128)} custom-call(f32[256,1024]{1,0:T(8,128)} %x_ref.1, f32[2,5,32,256]{3,2,1,0:T(8,128)} %bitcast.2, f32[2,32,256]{2,1,0:T(8,128)} %bitcast.3), custom_call_target="tpu_custom_call" | custom-call | tf_op jit(solution)/shard_map/panels/pallas_call | solution.py:481
  217.7 2.3 %copy.5 = f32[256,1024]{1,0:T(8,128)} copy(f32[256,1024]{1,0:T(8,128)} %panels.1) | data formatting | bytes 2097152
